TPU v7x, 32 devices: a whole 2x2x4 slice. The times are simulated.
32 devices in a mesh: ens: 2 (over x), lon: 8 (over z, y), lat: 2 (over core).
Axes of the slice: x: 2, y: 2, z: 4, core: 2. Of those that a mesh axis runs over, the one named last changes fastest.
Arguments:
- stream: float32 [6, 4, 24, 96, 512], P('ens', None, 'lat', 'lon'), parts along dimension 0, may hold values from -6 to 6
- region_ids: int32 [8, 24, 96], P('ens', 'lat', 'lon'), parts along dimension 0, may hold values from 0 to 2, as said below
- qkv_weight: bfloat16 [2, 512, 1536], replicated, may hold values from -0.25 to 0.25
- out_weight: bfloat16 [2, 512, 512], replicated, may hold values from -0.25 to 0.25
- up_weight: bfloat16 [2, 512, 2048], replicated, may hold values from -0.25 to 0.25
- down_weight: bfloat16 [2, 2048, 512], replicated, may hold values from -0.125 to 0.125
- norm_gain: float32 [2, 2, 512], replicated, may hold values from 0.5 to 1.5
- norm_bias: float32 [2, 2, 512], replicated, may hold values from -2 to 2
- logit_scale: float32 [2, 8], replicated, may hold values from 2 to 12
Outputs:
- mixed: float32 [6, 4, 24, 96, 512], P('ens', None, 'lat', 'lon'), parts along dimension 0
There are 2 independent parts, one for each index of `ens`. A program takes and returns all parts, laid end to end along the dimension named above; an argument that names none is the same for every part. Nothing has to cross between parts.
Inputs may be any that keep to these rules, and one draw needn't show every extreme that they name: `region_ids`: within each window of the rolled frame the ids depend only on the longitude column: they are 0, 1, 2 in three contiguous runs of columns, each run one column or more, the same over all levels and latitude rows of the window.
All inputs are finite; a program needn't handle non-finite values.
Results may differ from a plain program's by a relative error of at most 0.008.
Values may be sent and summed in bfloat16 or wider, within the bound.
A program may use at most 128 MiB of HBM per device.

v0:
```python
import functools

import jax
import jax.numpy as jnp
from jax import lax
from jax.experimental import pallas as pl
from jax.experimental.pallas import tpu as pltpu
from jax.sharding import PartitionSpec as P

WIN_LAT = 6
WIN_LON = 12
HALF_LAT = WIN_LAT // 2
HALF_LON = WIN_LON // 2
LOG2E = 1.4426950408889634
VMEM_LIMIT = 60 * 1024 * 1024

f32 = jnp.float32
bf16 = jnp.bfloat16


MESH = pl.DeviceIdType.MESH


def mm(a, b):
    return jnp.dot(a, b, preferred_element_type=f32)


def attend_window(operand, qkv_weight, scale_row, bias_ref, head_dim, store):
    tokens, width = operand.shape
    group = 4 * head_dim
    pair = 2 * head_dim
    rest = pair // 4
    main = tokens - rest
    last = (((1,), (1,)), ((), ()))
    query = mm(operand, qkv_weight[:, :width])
    key = mm(operand, qkv_weight[:, width : 2 * width])
    value = mm(operand, qkv_weight[:, 2 * width :]).astype(bf16)
    d0 = lax.broadcasted_iota(jnp.int32, (group, group), 0)
    d1 = lax.broadcasted_iota(jnp.int32, (group, group), 1)
    same_head = lax.shift_right_logical(d0, head_dim.bit_length() - 1) == lax.shift_right_logical(
        d1, head_dim.bit_length() - 1
    )
    same_head = same_head.astype(f32).astype(bf16)

    def lanes(rows, cols, at, size):
        lane = lax.broadcasted_iota(jnp.int32, (rows, cols), 1)
        return ((lane >= at) & (lane < at + size)).astype(f32).astype(bf16)

    first_b = lanes(tokens, pair, 0, head_dim)
    second_b = lanes(tokens, pair, head_dim, head_dim)
    first = lax.broadcasted_iota(jnp.int32, (tokens, pair), 1) < head_dim

    def unit(part, scale):
        rounded = part.astype(bf16)
        inv = lax.rsqrt(mm(rounded * rounded, same_head) + 1e-06)
        if scale is not None:
            inv = inv * scale
        return (part * inv).astype(bf16)

    for g in range(width // group):
        at = g * group
        q = unit(query[:, at : at + group], scale_row[:, at : at + group])
        k = unit(key[:, at : at + group], None)
        v = value[:, at : at + group]
        k_rest = jnp.concatenate(
            [k[main:] * lanes(rest, group, h * head_dim, head_dim) for h in range(4)], axis=0
        )
        rest_score = lax.dot_general(q, k_rest, last, preferred_element_type=f32)
        if bias_ref is not None:
            rest_score = rest_score + bias_ref[:, main:]
        rest_weights = jnp.exp2(rest_score).astype(bf16)
        columns = []
        for h in range(4):
            side = h % 2
            own, other = (first_b, second_b)[side][:rest], (second_b, first_b)[side][:rest]
            v_rest = v[main:, (h // 2) * pair : (h // 2 + 1) * pair] * own + other
            zero = jnp.zeros_like(v_rest)
            columns.append(jnp.concatenate([v_rest if i == h else zero for i in range(4)], axis=0))
        rest_out = mm(rest_weights, jnp.concatenate(columns, axis=1))
        shares = []
        for h in range(4):
            cut = slice((h // 2) * pair, (h // 2 + 1) * pair)
            own = (first_b, second_b)[h % 2][:main]
            score = lax.dot_general(q[:, cut], k[:main, cut] * own, last, preferred_element_type=f32)
            if bias_ref is not None:
                score = score + bias_ref[:, :main]
            shares.append(jnp.exp2(score).astype(bf16))
        for p in range(2):
            cut = slice(p * pair, (p + 1) * pair)
            v_pair = v[:main, cut]
            both = []
            for side, (own, other) in enumerate(((first_b, second_b), (second_b, first_b))):
                h = 2 * p + side
                both.append(
                    mm(shares[h], v_pair * own[:main] + other[:main]) + rest_out[:, h * pair : (h + 1) * pair]
                )
            result = jnp.where(first, both[0], both[1])
            total = pltpu.roll(jnp.where(first, both[1], both[0]), head_dim, 1)
            store(slice(at + p * pair, at + (p + 1) * pair), (result / total).astype(bf16))


def scale_lanes(scale_ref, layer, width, heads):
    lane = lax.broadcasted_iota(jnp.int32, (1, width), 1)
    row = jnp.zeros((1, width), f32)
    for h in range(heads):
        row = jnp.where(lane >= h * (width // heads), scale_ref[layer, h] * LOG2E, row)
    return row


def norm_rows(values, gain_row, bias_row):
    average = jnp.mean(values, -1, keepdims=True)
    centred = values - average
    spread = jnp.mean(centred * centred, -1, keepdims=True)
    return centred * (lax.rsqrt(spread + 1e-05)) * gain_row + bias_row


def gelu_twice(x):
    c = 0.7978845608028654
    x = x.astype(bf16)
    one = jnp.ones((), bf16)
    inner = x * (jnp.asarray(c, bf16) + jnp.asarray(c * 0.044715, bf16) * (x * x))
    return x * (one + jnp.tanh(inner))


def finish_window(x, attended, out_weight, up_ref, down_ref, gain, bias):
    after = x + norm_rows(mm(attended, out_weight), gain[0:1], bias[0:1])
    after_b = after.astype(bf16)
    ff = up_ref.shape[1]
    step = min(512, ff)
    total = None
    for at in range(0, ff, step):
        hidden = gelu_twice(mm(after_b, up_ref[:, at : at + step]))
        part = mm(hidden, down_ref[at : at + step, :])
        total = part if total is None else total + part
    return after + norm_rows(0.5 * total, gain[1:2], bias[1:2])


def window_keys(ids_ref, j, cols, main, rest, levels, base, lat_total):
    run = HALF_LON * levels
    quarter = HALF_LAT * run
    shape = (1, cols)
    at = lax.broadcasted_iota(jnp.int32, shape, 1)
    t = jnp.where(at < main, at, main + ((at - main) & (rest - 1))).astype(f32)

    def cut(value, by):
        return jnp.floor((value + 0.5) * (1.0 / by))

    q = cut(t, quarter)
    half = cut(q, 2)
    block = q - 2 * half
    inside = t - quarter * q
    r = cut(inside, run)
    column = half * HALF_LON + cut(inside - run * r, levels)
    row = base + block * HALF_LAT + r
    key = jnp.zeros(shape, f32)
    ids = ids_ref[j * WIN_LAT, 0:1, :].astype(f32)
    for c in range(WIN_LON):
        key = jnp.where(column == c, ids[:, c : c + 1], key)
    band = jnp.where(row >= lat_total - WIN_LAT, 1.0, 0.0) + jnp.where(row >= lat_total - HALF_LAT, 1.0, 0.0)
    return key * 3 + band


def kernel(lat_size, x_hbm, ids_ref, qkv_hbm, out_hbm, up_hbm, down_hbm, gain_ref, bias_ref, scale_ref,
           y_hbm, x_s, first_s, op_s, att_s, send_s, send_own, back_s, back_own, mask_s, win_f, win_b,
           scale_s, qkv_s, out_s, up_s, down_s, w_sem, x_sem, y_sem, send1, recv1, send2, recv2):
    samples, lat_rows, lon_cols, levels, width = x_s.shape
    wins = lat_rows // WIN_LAT
    blocks = 2 * wins
    run = HALF_LON * levels
    quarter = HALF_LAT * run
    last_block = blocks - 1

    loads = [
        [
            pltpu.make_async_copy(src.at[layer], dst.at[layer], w_sem.at[layer, k])
            for k, (src, dst) in enumerate(
                ((qkv_hbm, qkv_s), (out_hbm, out_s), (up_hbm, up_s), (down_hbm, down_s))
            )
        ]
        for layer in range(2)
    ]

    def x_load(s):
        return pltpu.make_async_copy(x_hbm.at[s], x_s.at[s], x_sem.at[s])

    x_load(0).start()
    for copy in loads[0]:
        copy.start()
    for s in range(1, samples):
        x_load(s).start()
    for copy in loads[1]:
        copy.start()

    lon, lat = lax.axis_index("lon"), lax.axis_index("lat")
    lon_size = lax.axis_size("lon")
    west = lax.rem(lon + lon_size - 1, lon_size)
    east = lax.rem(lon + 1, lon_size)
    before = lax.rem(lat + lat_size - 1, lat_size)
    after = lax.rem(lat + 1, lat_size)

    barrier = pltpu.get_barrier_semaphore()
    peers = ((west, lat), (west, before), (lon, before), (lon, after), (east, lat), (east, after))
    for to_lon, to_lat in peers:
        pl.semaphore_signal(barrier, inc=1, device_id={"lon": to_lon, "lat": to_lat}, device_id_type=MESH)
    pl.semaphore_wait(barrier, len(peers))

    heads = scale_ref.shape[1]
    head_dim = width // heads
    rest = head_dim // 2
    tokens = 4 * quarter
    for layer in range(2):
        scale_s[layer : layer + 1, :] = scale_lanes(scale_ref, layer, width, heads)

    lat_total = lat_size * lat_rows
    cols = tokens + 3 * rest
    for j in range(wins):
        base = (lat * lat_rows + j * WIN_LAT).astype(f32)
        key = window_keys(ids_ref, j, cols, tokens - rest, rest, levels, base, lat_total)
        kinds = lax.broadcasted_iota(jnp.int32, (16, cols), 0).astype(f32)
        member = (kinds == key).astype(f32).astype(bf16)
        same = lax.dot_general(member[:, :tokens], member, (((0,), (0,)), ((), ())), preferred_element_type=f32)
        mask_s[j] = (same - 1.0) * 1e30

    def remote(src, dst, send, recv, to_lon, to_lat):
        return pltpu.make_async_remote_copy(
            src_ref=src, dst_ref=dst, send_sem=send, recv_sem=recv,
            device_id={"lon": to_lon, "lat": to_lat}, device_id_type=MESH,
        )

    def ahead(s, k):
        if k == 0:
            return remote(send_s.at[s, pl.ds(1, 1)], op_s.at[s, 1, pl.ds(0, 1)], send1.at[s, k], recv1.at[s, k], west, lat)
        if k == 1:
            return remote(send_s.at[s, pl.ds(0, 1)], op_s.at[s, 1, pl.ds(last_block, 1)], send1.at[s, k], recv1.at[s, k], west, before)
        if k == 2:
            return remote(send_own.at[s], op_s.at[s, 0, pl.ds(last_block, 1)], send1.at[s, k], recv1.at[s, k], lon, before)
        j = k - 2
        return remote(send_s.at[s, pl.ds(2 * j, 2)], op_s.at[s, 1, pl.ds(2 * j - 1, 2)], send1.at[s, k], recv1.at[s, k], west, lat)

    def back(s, k):
        if k == 0:
            return remote(back_s.at[s, pl.ds(last_block - 1, 1)], att_s.at[s, 0, pl.ds(last_block, 1)], send2.at[s, k], recv2.at[s, k], east, lat)
        if k == 1:
            return remote(back_s.at[s, pl.ds(last_block, 1)], att_s.at[s, 0, pl.ds(0, 1)], send2.at[s, k], recv2.at[s, k], east, after)
        if k == 2:
            return remote(back_own.at[s], att_s.at[s, 1, pl.ds(0, 1)], send2.at[s, k], recv2.at[s, k], lon, after)
        j = k - 3
        return remote(back_s.at[s, pl.ds(2 * j, 2)], att_s.at[s, 0, pl.ds(2 * j + 1, 2)], send2.at[s, k], recv2.at[s, k], east, lat)

    copies = 3 + wins - 1

    def store(cut, value):
        win_b[:, cut] = value

    def layer_first(i, carry):
        s, j = lax.div(i, wins), lax.rem(i, wins)

        @pl.when(j == 0)
        def _():
            x_load(s).wait()

        @pl.when(i == 0)
        def _():
            loads[0][0].wait()

        for half in range(2):
            for block in range(2):
                for r in range(HALF_LAT):
                    row = (half * 2 + block) * quarter + r * run
                    part = x_s[s, j * WIN_LAT + block * HALF_LAT + r, half * HALF_LON : (half + 1) * HALF_LON]
                    first_s[i, row : row + run, :] = part.reshape(run, width)
        attend_window(first_s[i].astype(bf16), qkv_s.at[0], scale_s[0:1, :], None, head_dim, store)

        @pl.when(i == 0)
        def _():
            for copy in loads[0][1:]:
                copy.wait()

        first_s[i] = finish_window(first_s[i], win_b[...], out_s[0], up_s.at[0], down_s.at[0], gain_ref[0], bias_ref[0])

        def block_of(q):
            return first_s[i, q * quarter : (q + 1) * quarter, :].astype(bf16)

        send_s[s, 2 * j] = block_of(0)
        send_s[s, 2 * j + 1] = block_of(1)
        op_s[s, 0, 2 * j] = block_of(3)

        @pl.when(j == 0)
        def _():
            send_own[s, 0] = block_of(2)
            for k in range(3):
                ahead(s, k).start()

        for jj in range(1, wins):

            @pl.when(j == jj)
            def _():
                op_s[s, 0, 2 * jj - 1] = block_of(2)
                ahead(s, 2 + jj).start()

        return carry

    def shifted_attention(i, carry):
        s, j = lax.div(i, wins), lax.rem(i, wins)

        @pl.when(j == 0)
        def _():
            for k in range(copies):
                ahead(s, k).wait_recv()

        @pl.when(i == 0)
        def _():
            loads[1][0].wait()

        for half in range(2):
            for block in range(2):
                row = (half * 2 + block) * quarter
                win_f[row : row + quarter, :] = op_s[s, half, 2 * j + block].astype(f32)
        attend_window(win_f[...].astype(bf16), qkv_s.at[1], scale_s[1:2, :], mask_s.at[j], head_dim, store)
        win_f[...] = win_b[...].astype(f32)

        def block_of(q):
            return win_f[q * quarter : (q + 1) * quarter, :].astype(bf16)

        att_s[s, 1, 2 * j + 1] = block_of(0)
        back_s[s, 2 * j] = block_of(2)
        back_s[s, 2 * j + 1] = block_of(3)

        @pl.when(j == wins - 1)
        def _():
            back_own[s, 0] = block_of(1)
            for k in range(3):
                back(s, k).start()

        for jj in range(wins - 1):

            @pl.when(j == jj)
            def _():
                att_s[s, 1, 2 * jj + 2] = block_of(1)
                back(s, 3 + jj).start()

        return carry

    def y_copy(s, j):
        rows = pl.ds(j * WIN_LAT, WIN_LAT)
        return pltpu.make_async_copy(x_s.at[s, rows], y_hbm.at[s, rows], y_sem.at[s, j])

    def layer_last(i, carry):
        s, j = lax.div(i, wins), lax.rem(i, wins)

        @pl.when(j == 0)
        def _():
            for k in range(copies):
                back(s, k).wait_recv()

        @pl.when(i == 0)
        def _():
            for copy in loads[1][1:]:
                copy.wait()

        for half in range(2):
            for block in range(2):
                row = (half * 2 + block) * quarter
                win_f[row : row + quarter, :] = att_s[s, half, 2 * j + block].astype(f32)
        win_f[...] = finish_window(
            first_s[i], win_f[...].astype(bf16), out_s[1], up_s.at[1], down_s.at[1], gain_ref[1], bias_ref[1]
        )
        for half in range(2):
            for block in range(2):
                for r in range(HALF_LAT):
                    row = (half * 2 + block) * quarter + r * run
                    x_s[s, j * WIN_LAT + block * HALF_LAT + r, half * HALF_LON : (half + 1) * HALF_LON] = win_f[
                        row : row + run, :
                    ].reshape(HALF_LON, levels, width)
        y_copy(s, j).start()
        return carry

    def stage(k, carry):
        for lag, step in enumerate((layer_first, shifted_attention, layer_last)):
            s = k - lag

            @pl.when((s >= 0) & (s < samples))
            def _():
                lax.fori_loop(s * wins, (s + 1) * wins, step, 0)

        return carry

    lax.fori_loop(0, samples + 2, stage, 0)

    def drain(s, carry):
        for k in range(copies):
            ahead(s, k).wait_send()
            back(s, k).wait_send()
        for j in range(wins):
            y_copy(s, j).wait()
        return carry

    lax.fori_loop(0, samples, drain, 0)


def local(stream, region_ids, qkv_weight, out_weight, up_weight, down_weight, norm_gain, norm_bias, logit_scale):
    samples, levels, lat_rows, lon_cols, width = stream.shape
    assert lon_cols == WIN_LON
    wins = lat_rows // WIN_LAT
    blocks = 2 * wins
    quarter = levels * HALF_LAT * HALF_LON
    tokens = 4 * quarter
    copies = 3 + wins - 1
    x = stream.transpose(0, 2, 3, 1, 4)
    ids = region_ids.transpose(1, 0, 2)
    hbm = pl.BlockSpec(memory_space=pl.ANY)
    vmem = pl.BlockSpec(memory_space=pltpu.VMEM)
    smem = pl.BlockSpec(memory_space=pltpu.SMEM)
    sem = pltpu.SemaphoreType.DMA
    y = pl.pallas_call(
        functools.partial(kernel, lax.axis_size("lat")),
        in_specs=[hbm, vmem, hbm, hbm, hbm, hbm, vmem, vmem, smem],
        out_specs=hbm,
        out_shape=jax.ShapeDtypeStruct(x.shape, f32),
        scratch_shapes=[
            pltpu.VMEM(x.shape, f32),
            pltpu.VMEM((samples * wins, tokens, width), f32),
            pltpu.VMEM((samples, 2, blocks, quarter, width), bf16),
            pltpu.VMEM((samples, 2, blocks, quarter, width), bf16),
            pltpu.VMEM((samples, blocks, quarter, width), bf16),
            pltpu.VMEM((samples, 1, quarter, width), bf16),
            pltpu.VMEM((samples, blocks, quarter, width), bf16),
            pltpu.VMEM((samples, 1, quarter, width), bf16),
            pltpu.VMEM((wins, tokens, tokens + 3 * (width // logit_scale.shape[1] // 2)), f32),
            pltpu.VMEM((tokens, width), f32),
            pltpu.VMEM((tokens, width), bf16),
            pltpu.VMEM((2, width), f32),
            pltpu.VMEM(qkv_weight.shape, bf16),
            pltpu.VMEM(out_weight.shape, bf16),
            pltpu.VMEM(up_weight.shape, bf16),
            pltpu.VMEM(down_weight.shape, bf16),
            sem((2, 4)),
            sem((samples,)),
            sem((samples, wins)),
            sem((samples, copies)),
            sem((samples, copies)),
            sem((samples, copies)),
            sem((samples, copies)),
        ],
        compiler_params=pltpu.CompilerParams(
            vmem_limit_bytes=VMEM_LIMIT, collective_id=0, has_side_effects=True
        ),
        name="both_layers",
    )(x, ids, qkv_weight, out_weight, up_weight, down_weight, norm_gain, norm_bias, logit_scale)
    return y.transpose(0, 3, 1, 2, 4)


def solution(mesh):
    in_specs = (P("ens", None, "lat", "lon", None), P("ens", "lat", "lon")) + (P(),) * 7
    out_specs = P("ens", None, "lat", "lon", None)
    return jax.shard_map(local, mesh=mesh, in_specs=in_specs, out_specs=out_specs, check_vma=False)
```

profile of v0, /device:TPU:1, one launch (start us, length us, event | category | flops | bytes accessed | tf_op | source)
XLA Modules:
  0.0 71.5 jit_solution(17548798208560574217)
XLA Ops:
  0.0 66.7 %both_layers.1 = f32[3,12,12,4,512]{4,3,2,1,0:T(4,128)} custom-call(f32[3,12,12,4,512]{4,3,2,1,0:T(4,128)} %bitcast.4, s32[12,4,12]{2,1,0:T(4,128)} %bitcast.5, bf16[2,512,1536]{2,1,0:T(8,128)(2,1)} %qkv_hbm.1, bf16[2,512,512]{2,1,0:T(8,128)(2,1)} %out_hbm.1, bf16[2,512,2048]{2,1,0:T(8,128)(2,1)} %up_hbm.1, bf16[2,2048,512]{2,1,0:T(8,128)(2,1)} %down_hbm.1, ...), custom_call_target="tpu_custom_call" | custom-call | tf_op jit(solution)/shard_map/both_layers/pallas_call | solution.py:415
  66.7 4.8 %copy.11 = f32[3,4,12,12,512]{4,1,3,2,0:T(4,128)} copy(f32[3,4,12,12,512]{4,1,3,2,0:T(4,128)} %bitcast.3) | data formatting | bytes 7077888
where the time goes:
time: 71.7 us; the launch traced here: 71.5 us
  Pallas kernels  66.7 us (93%)
  local copies, waits for them, and re-layouts  4.79 us (7%)
    pallas_call x1, Pallas kernels, local(): pl.pallas_call(functools.partial(kernel, lax.axis_size('lat')), in_specs=...  66.7 us
    unnamed x1, local copies, waits for them, and re-layouts  4.79 us

commit v1 on v0

--- a/solution.py
+++ b/solution.py
@@ -202,7 +202,6 @@
     peers = ((west, lat), (west, before), (lon, before), (lon, after), (east, lat), (east, after))
     for to_lon, to_lat in peers:
         pl.semaphore_signal(barrier, inc=1, device_id={"lon": to_lon, "lat": to_lat}, device_id_type=MESH)
-    pl.semaphore_wait(barrier, len(peers))
 
     heads = scale_ref.shape[1]
     head_dim = width // heads
@@ -280,6 +279,10 @@
 
         def block_of(q):
             return first_s[i, q * quarter : (q + 1) * quarter, :].astype(bf16)
+
+        @pl.when(i == 0)
+        def _():
+            pl.semaphore_wait(barrier, len(peers))
 
         send_s[s, 2 * j] = block_of(0)
         send_s[s, 2 * j + 1] = block_of(1)

time: 71.7 us -> 71.9 us (level)
  no operation moved by 1% of the time
where the time goes in v1:
time: 71.9 us; the launch traced here: 71.7 us
  Pallas kernels  66.9 us (93%)
  local copies, waits for them, and re-layouts  4.79 us (7%)
    pallas_call x1, Pallas kernels, local(): pl.pallas_call(functools.partial(kernel, lax.axis_size('lat')), in_specs=...  66.9 us
    unnamed x1, local copies, waits for them, and re-layouts  4.79 us

profile of v1, /device:TPU:1, one launch (start us, length us, event | category | flops | bytes accessed | tf_op | source)
XLA Modules:
  0.0 71.7 jit_solution(8741249806733878496)
XLA Ops:
  0.0 66.9 %both_layers.1 = f32[3,12,12,4,512]{4,3,2,1,0:T(4,128)} custom-call(f32[3,12,12,4,512]{4,3,2,1,0:T(4,128)} %bitcast.4, s32[12,4,12]{2,1,0:T(4,128)} %bitcast.5, bf16[2,512,1536]{2,1,0:T(8,128)(2,1)} %qkv_hbm.1, bf16[2,512,512]{2,1,0:T(8,128)(2,1)} %out_hbm.1, bf16[2,512,2048]{2,1,0:T(8,128)(2,1)} %up_hbm.1, bf16[2,2048,512]{2,1,0:T(8,128)(2,1)} %down_hbm.1, ...), custom_call_target="tpu_custom_call" | custom-call | tf_op jit(solution)/shard_map/both_layers/pallas_call | solution.py:418
  66.9 4.8 %copy.11 = f32[3,4,12,12,512]{4,1,3,2,0:T(4,128)} copy(f32[3,4,12,12,512]{4,1,3,2,0:T(4,128)} %bitcast.3) | data formatting | bytes 7077888

commit v2 on v1

--- a/solution.py
+++ b/solution.py
@@ -378,17 +378,8 @@
         y_copy(s, j).start()
         return carry
 
-    def stage(k, carry):
-        for lag, step in enumerate((layer_first, shifted_attention, layer_last)):
-            s = k - lag
-
-            @pl.when((s >= 0) & (s < samples))
-            def _():
-                lax.fori_loop(s * wins, (s + 1) * wins, step, 0)
-
-        return carry
-
-    lax.fori_loop(0, samples + 2, stage, 0)
+    for step in (layer_first, shifted_attention, layer_last):
+        lax.fori_loop(0, samples * wins, step, 0)
 
     def drain(s, carry):
         for k in range(copies):

time: 71.9 us -> 81.1 us (1.13)
  the two profiles are of different devices: /device:TPU:1 before, /device:TPU:26 now
where the time goes in v2:
time: 81.1 us; the launch traced here: 80.9 us
  Pallas kernels  76.1 us (94%)
  local copies, waits for them, and re-layouts  4.79 us (6%)
    pallas_call x1, Pallas kernels, local(): pl.pallas_call(functools.partial(kernel, lax.axis_size('lat')), in_specs=...  76.1 us
    unnamed x1, local copies, waits for them, and re-layouts  4.79 us

profile of v2, /device:TPU:26, one launch (start us, length us, event | category | flops | bytes accessed | tf_op | source)
XLA Modules:
  0.0 80.9 jit_solution(7037776752481066170)
XLA Ops:
  0.0 76.1 %both_layers.1 = f32[3,12,12,4,512]{4,3,2,1,0:T(4,128)} custom-call(f32[3,12,12,4,512]{4,3,2,1,0:T(4,128)} %bitcast.4, s32[12,4,12]{2,1,0:T(4,128)} %bitcast.5, bf16[2,512,1536]{2,1,0:T(8,128)(2,1)} %qkv_hbm.1, bf16[2,512,512]{2,1,0:T(8,128)(2,1)} %out_hbm.1, bf16[2,512,2048]{2,1,0:T(8,128)(2,1)} %up_hbm.1, bf16[2,2048,512]{2,1,0:T(8,128)(2,1)} %down_hbm.1, ...), custom_call_target="tpu_custom_call" | custom-call | tf_op jit(solution)/shard_map/both_layers/pallas_call | solution.py:409
  76.2 4.8 %copy.11 = f32[3,4,12,12,512]{4,1,3,2,0:T(4,128)} copy(f32[3,4,12,12,512]{4,1,3,2,0:T(4,128)} %bitcast.3) | data formatting | bytes 7077888

commit v3 on v2

--- a/solution.py
+++ b/solution.py
@@ -160,9 +160,22 @@
     return key * 3 + band
 
 
+ORDER = "FFFFSSFFSSLLSSLLLL"
+
+
+def order(count):
+    seen = {"F": 0, "S": 0, "L": 0}
+    plan = []
+    for kind in ORDER:
+        plan.append(("FSL".index(kind), seen[kind]))
+        seen[kind] += 1
+    assert min(seen.values()) == max(seen.values()) == count
+    return plan
+
+
 def kernel(lat_size, x_hbm, ids_ref, qkv_hbm, out_hbm, up_hbm, down_hbm, gain_ref, bias_ref, scale_ref,
-           y_hbm, x_s, first_s, op_s, att_s, send_s, send_own, back_s, back_own, mask_s, win_f, win_b,
-           scale_s, qkv_s, out_s, up_s, down_s, w_sem, x_sem, y_sem, send1, recv1, send2, recv2):
+           x_s, first_s, op_s, att_s, send_s, send_own, back_s, back_own, mask_s, win_f, win_b,
+           scale_s, qkv_s, out_s, up_s, down_s, w_sem, x_sem, send1, recv1, send2, recv2):
     samples, lat_rows, lon_cols, levels, width = x_s.shape
     wins = lat_rows // WIN_LAT
     blocks = 2 * wins
@@ -343,10 +356,6 @@
                 back(s, 3 + jj).start()
 
         return carry
-
-    def y_copy(s, j):
-        rows = pl.ds(j * WIN_LAT, WIN_LAT)
-        return pltpu.make_async_copy(x_s.at[s, rows], y_hbm.at[s, rows], y_sem.at[s, j])
 
     def layer_last(i, carry):
         s, j = lax.div(i, wins), lax.rem(i, wins)
@@ -375,18 +384,34 @@
                     x_s[s, j * WIN_LAT + block * HALF_LAT + r, half * HALF_LON : (half + 1) * HALF_LON] = win_f[
                         row : row + run, :
                     ].reshape(HALF_LON, levels, width)
-        y_copy(s, j).start()
         return carry
 
-    for step in (layer_first, shifted_attention, layer_last):
-        lax.fori_loop(0, samples * wins, step, 0)
+    plan = order(samples * wins)
+
+    def pick(t, values):
+        value = jnp.int32(values[0])
+        for n in range(1, len(values)):
+            if values[n] != values[n - 1]:
+                value = jnp.where(t >= n, jnp.int32(values[n]), value)
+        return value
+
+    def advance(t, carry):
+        kind = pick(t, [k for k, _ in plan])
+        i = pick(t, [n for _, n in plan])
+        for k, step in enumerate((layer_first, shifted_attention, layer_last)):
+
+            @pl.when(kind == k)
+            def _():
+                step(i, 0)
+
+        return carry
+
+    lax.fori_loop(0, len(plan), advance, 0)
 
     def drain(s, carry):
         for k in range(copies):
             ahead(s, k).wait_send()
             back(s, k).wait_send()
-        for j in range(wins):
-            y_copy(s, j).wait()
         return carry
 
     lax.fori_loop(0, samples, drain, 0)
@@ -409,10 +434,9 @@
     y = pl.pallas_call(
         functools.partial(kernel, lax.axis_size("lat")),
         in_specs=[hbm, vmem, hbm, hbm, hbm, hbm, vmem, vmem, smem],
-        out_specs=hbm,
-        out_shape=jax.ShapeDtypeStruct(x.shape, f32),
+        out_specs=vmem,
+        out_shape=pltpu.VMEM(x.shape, f32),
         scratch_shapes=[
-            pltpu.VMEM(x.shape, f32),
             pltpu.VMEM((samples * wins, tokens, width), f32),
             pltpu.VMEM((samples, 2, blocks, quarter, width), bf16),
             pltpu.VMEM((samples, 2, blocks, quarter, width), bf16),
@@ -430,7 +454,6 @@
             pltpu.VMEM(down_weight.shape, bf16),
             sem((2, 4)),
             sem((samples,)),
-            sem((samples, wins)),
             sem((samples, copies)),
             sem((samples, copies)),
             sem((samples, copies)),

time: 81.1 us -> 68.3 us (0.84)
  the two profiles are of different devices: /device:TPU:26 before, /device:TPU:1 now
where the time goes in v3:
time: 68.3 us; the launch traced here: 68.2 us
  Pallas kernels  66.3 us (97%)
  local copies, waits for them, and re-layouts  1.8 us (3%)
    pallas_call x1, Pallas kernels, local(): pl.pallas_call(functools.partial(kernel, lax.axis_size('lat')), in_specs=...  66.3 us
    unnamed x1, local copies, waits for them, and re-layouts  1.8 us

profile of v3, /device:TPU:1, one launch (start us, length us, event | category | flops | bytes accessed | tf_op | source)
XLA Modules:
  0.0 68.2 jit_solution(4289239777754927586)
XLA Ops:
  0.0 66.3 %both_layers.1 = f32[3,12,12,4,512]{4,3,2,1,0:T(4,128)S(1)} custom-call(f32[3,12,12,4,512]{4,3,2,1,0:T(4,128)} %bitcast.4, s32[12,4,12]{2,1,0:T(4,128)} %bitcast.5, bf16[2,512,1536]{2,1,0:T(8,128)(2,1)} %qkv_hbm.1, bf16[2,512,512]{2,1,0:T(8,128)(2,1)} %out_hbm.1, bf16[2,512,2048]{2,1,0:T(8,128)(2,1)} %up_hbm.1, bf16[2,2048,512]{2,1,0:T(8,128)(2,1)} %down_hbm.1, ...), custom_call_target="tpu_custom_call" | custom-call | tf_op jit(solution)/shard_map/both_layers/pallas_call | solution.py:434
  66.4 1.8 %copy.11 = f32[3,4,12,12,512]{4,1,3,2,0:T(4,128)} copy(f32[3,4,12,12,512]{4,1,3,2,0:T(4,128)S(1)} %bitcast.3) | data formatting | bytes 7077888

commit v4 on v3

--- a/solution.py
+++ b/solution.py
@@ -175,7 +175,7 @@
 
 def kernel(lat_size, x_hbm, ids_ref, qkv_hbm, out_hbm, up_hbm, down_hbm, gain_ref, bias_ref, scale_ref,
            x_s, first_s, op_s, att_s, send_s, send_own, back_s, back_own, mask_s, win_f, win_b,
-           scale_s, qkv_s, out_s, up_s, down_s, w_sem, x_sem, send1, recv1, send2, recv2):
+           scale_s, qkv_s, out_s, up_s, down_s, w_sem, x_sem, send1, recv1, send2, recv2, ids_s, ids_sem):
     samples, lat_rows, lon_cols, levels, width = x_s.shape
     wins = lat_rows // WIN_LAT
     blocks = 2 * wins
@@ -212,7 +212,7 @@
     after = lax.rem(lat + 1, lat_size)
 
     barrier = pltpu.get_barrier_semaphore()
-    peers = ((west, lat), (west, before), (lon, before), (lon, after), (east, lat), (east, after))
+    peers = ((east, lat), (east, before), (lon, before), (lon, after), (west, lat), (west, after))
     for to_lon, to_lat in peers:
         pl.semaphore_signal(barrier, inc=1, device_id={"lon": to_lon, "lat": to_lat}, device_id_type=MESH)
 
@@ -223,16 +223,6 @@
     for layer in range(2):
         scale_s[layer : layer + 1, :] = scale_lanes(scale_ref, layer, width, heads)
 
-    lat_total = lat_size * lat_rows
-    cols = tokens + 3 * rest
-    for j in range(wins):
-        base = (lat * lat_rows + j * WIN_LAT).astype(f32)
-        key = window_keys(ids_ref, j, cols, tokens - rest, rest, levels, base, lat_total)
-        kinds = lax.broadcasted_iota(jnp.int32, (16, cols), 0).astype(f32)
-        member = (kinds == key).astype(f32).astype(bf16)
-        same = lax.dot_general(member[:, :tokens], member, (((0,), (0,)), ((), ())), preferred_element_type=f32)
-        mask_s[j] = (same - 1.0) * 1e30
-
     def remote(src, dst, send, recv, to_lon, to_lat):
         return pltpu.make_async_remote_copy(
             src_ref=src, dst_ref=dst, send_sem=send, recv_sem=recv,
@@ -241,23 +231,37 @@
 
     def ahead(s, k):
         if k == 0:
-            return remote(send_s.at[s, pl.ds(1, 1)], op_s.at[s, 1, pl.ds(0, 1)], send1.at[s, k], recv1.at[s, k], west, lat)
+            return remote(send_s.at[s, pl.ds(1, 1)], op_s.at[s, 0, pl.ds(0, 1)], send1.at[s, k], recv1.at[s, k], east, lat)
         if k == 1:
-            return remote(send_s.at[s, pl.ds(0, 1)], op_s.at[s, 1, pl.ds(last_block, 1)], send1.at[s, k], recv1.at[s, k], west, before)
+            return remote(send_s.at[s, pl.ds(0, 1)], op_s.at[s, 0, pl.ds(last_block, 1)], send1.at[s, k], recv1.at[s, k], east, before)
         if k == 2:
-            return remote(send_own.at[s], op_s.at[s, 0, pl.ds(last_block, 1)], send1.at[s, k], recv1.at[s, k], lon, before)
+            return remote(send_own.at[s], op_s.at[s, 1, pl.ds(last_block, 1)], send1.at[s, k], recv1.at[s, k], lon, before)
         j = k - 2
-        return remote(send_s.at[s, pl.ds(2 * j, 2)], op_s.at[s, 1, pl.ds(2 * j - 1, 2)], send1.at[s, k], recv1.at[s, k], west, lat)
+        return remote(send_s.at[s, pl.ds(2 * j, 2)], op_s.at[s, 0, pl.ds(2 * j - 1, 2)], send1.at[s, k], recv1.at[s, k], east, lat)
 
     def back(s, k):
         if k == 0:
-            return remote(back_s.at[s, pl.ds(last_block - 1, 1)], att_s.at[s, 0, pl.ds(last_block, 1)], send2.at[s, k], recv2.at[s, k], east, lat)
+            return remote(back_s.at[s, pl.ds(last_block - 1, 1)], att_s.at[s, 1, pl.ds(last_block, 1)], send2.at[s, k], recv2.at[s, k], west, lat)
         if k == 1:
-            return remote(back_s.at[s, pl.ds(last_block, 1)], att_s.at[s, 0, pl.ds(0, 1)], send2.at[s, k], recv2.at[s, k], east, after)
+            return remote(back_s.at[s, pl.ds(last_block, 1)], att_s.at[s, 1, pl.ds(0, 1)], send2.at[s, k], recv2.at[s, k], west, after)
         if k == 2:
-            return remote(back_own.at[s], att_s.at[s, 1, pl.ds(0, 1)], send2.at[s, k], recv2.at[s, k], lon, after)
+            return remote(back_own.at[s], att_s.at[s, 0, pl.ds(0, 1)], send2.at[s, k], recv2.at[s, k], lon, after)
         j = k - 3
-        return remote(back_s.at[s, pl.ds(2 * j, 2)], att_s.at[s, 0, pl.ds(2 * j + 1, 2)], send2.at[s, k], recv2.at[s, k], east, lat)
+        return remote(back_s.at[s, pl.ds(2 * j, 2)], att_s.at[s, 1, pl.ds(2 * j + 1, 2)], send2.at[s, k], recv2.at[s, k], west, lat)
+
+    def ids_copy():
+        return remote(ids_ref, ids_s, ids_sem.at[0], ids_sem.at[1], east, lat)
+
+    def make_masks():
+        lat_total = lat_size * lat_rows
+        cols = tokens + 3 * rest
+        for j in range(wins):
+            base = (lat * lat_rows + j * WIN_LAT).astype(f32)
+            key = window_keys(ids_s, j, cols, tokens - rest, rest, levels, base, lat_total)
+            kinds = lax.broadcasted_iota(jnp.int32, (16, cols), 0).astype(f32)
+            member = (kinds == key).astype(f32).astype(bf16)
+            same = lax.dot_general(member[:, :tokens], member, (((0,), (0,)), ((), ())), preferred_element_type=f32)
+            mask_s[j] = (same - 1.0) * 1e30
 
     copies = 3 + wins - 1
 
@@ -296,14 +300,15 @@
         @pl.when(i == 0)
         def _():
             pl.semaphore_wait(barrier, len(peers))
-
-        send_s[s, 2 * j] = block_of(0)
-        send_s[s, 2 * j + 1] = block_of(1)
-        op_s[s, 0, 2 * j] = block_of(3)
+            ids_copy().start()
+
+        send_s[s, 2 * j] = block_of(2)
+        send_s[s, 2 * j + 1] = block_of(3)
+        op_s[s, 1, 2 * j] = block_of(1)
 
         @pl.when(j == 0)
         def _():
-            send_own[s, 0] = block_of(2)
+            send_own[s, 0] = block_of(0)
             for k in range(3):
                 ahead(s, k).start()
 
@@ -311,7 +316,7 @@
 
             @pl.when(j == jj)
             def _():
-                op_s[s, 0, 2 * jj - 1] = block_of(2)
+                op_s[s, 1, 2 * jj - 1] = block_of(0)
                 ahead(s, 2 + jj).start()
 
         return carry
@@ -321,12 +326,24 @@
 
         @pl.when(j == 0)
         def _():
-            for k in range(copies):
+            ahead(s, 0).wait_recv()
+
+        for jj in range(1, wins):
+
+            @pl.when(j == jj - 1)
+            def _():
+                ahead(s, 2 + jj).wait_recv()
+
+        @pl.when(j == wins - 1)
+        def _():
+            for k in (1, 2):
                 ahead(s, k).wait_recv()
 
         @pl.when(i == 0)
         def _():
             loads[1][0].wait()
+            ids_copy().wait_recv()
+            make_masks()
 
         for half in range(2):
             for block in range(2):
@@ -338,13 +355,13 @@
         def block_of(q):
             return win_f[q * quarter : (q + 1) * quarter, :].astype(bf16)
 
-        att_s[s, 1, 2 * j + 1] = block_of(0)
-        back_s[s, 2 * j] = block_of(2)
-        back_s[s, 2 * j + 1] = block_of(3)
+        att_s[s, 0, 2 * j + 1] = block_of(2)
+        back_s[s, 2 * j] = block_of(0)
+        back_s[s, 2 * j + 1] = block_of(1)
 
         @pl.when(j == wins - 1)
         def _():
-            back_own[s, 0] = block_of(1)
+            back_own[s, 0] = block_of(3)
             for k in range(3):
                 back(s, k).start()
 
@@ -352,7 +369,7 @@
 
             @pl.when(j == jj)
             def _():
-                att_s[s, 1, 2 * jj + 2] = block_of(1)
+                att_s[s, 0, 2 * jj + 2] = block_of(3)
                 back(s, 3 + jj).start()
 
         return carry
@@ -362,8 +379,18 @@
 
         @pl.when(j == 0)
         def _():
-            for k in range(copies):
+            for k in (1, 2):
                 back(s, k).wait_recv()
+
+        for jj in range(wins - 1):
+
+            @pl.when(j == jj)
+            def _():
+                back(s, 3 + jj).wait_recv()
+
+        @pl.when(j == wins - 1)
+        def _():
+            back(s, 0).wait_recv()
 
         @pl.when(i == 0)
         def _():
@@ -415,6 +442,7 @@
         return carry
 
     lax.fori_loop(0, samples, drain, 0)
+    ids_copy().wait_send()
 
 
 def local(stream, region_ids, qkv_weight, out_weight, up_weight, down_weight, norm_gain, norm_bias, logit_scale):
@@ -458,6 +486,8 @@
             sem((samples, copies)),
             sem((samples, copies)),
             sem((samples, copies)),
+            pltpu.VMEM(ids.shape, jnp.int32),
+            sem((2,)),
         ],
         compiler_params=pltpu.CompilerParams(
             vmem_limit_bytes=VMEM_LIMIT, collective_id=0, has_side_effects=True

time: 68.3 us -> 65.6 us (0.960)
  Pallas kernels: 66.3 us -> 63.6 us
    pallas_call x1, Pallas kernels: 66.3 us -> 63.6 us  [local(): pl.pallas_call(functools.partial(kernel, lax.axis_size('lat')), in_specs=...]
where the time goes in v4:
time: 65.6 us; the launch traced here: 65.4 us
  Pallas kernels  63.6 us (97%)
  local copies, waits for them, and re-layouts  1.8 us (3%)
    pallas_call x1, Pallas kernels, local(): pl.pallas_call(functools.partial(kernel, lax.axis_size('lat')), in_specs=...  63.6 us
    unnamed x1, local copies, waits for them, and re-layouts  1.8 us

profile of v4, /device:TPU:1, one launch (start us, length us, event | category | flops | bytes accessed | tf_op | source)
XLA Modules:
  0.0 65.4 jit_solution(9695251254213093823)
XLA Ops:
  0.0 63.6 %both_layers.1 = f32[3,12,12,4,512]{4,3,2,1,0:T(4,128)S(1)} custom-call(f32[3,12,12,4,512]{4,3,2,1,0:T(4,128)} %bitcast.4, s32[12,4,12]{2,1,0:T(4,128)} %bitcast.5, bf16[2,512,1536]{2,1,0:T(8,128)(2,1)} %qkv_hbm.1, bf16[2,512,512]{2,1,0:T(8,128)(2,1)} %out_hbm.1, bf16[2,512,2048]{2,1,0:T(8,128)(2,1)} %up_hbm.1, bf16[2,2048,512]{2,1,0:T(8,128)(2,1)} %down_hbm.1, ...), custom_call_target="tpu_custom_call" | custom-call | tf_op jit(solution)/shard_map/both_layers/pallas_call | solution.py:462
  63.6 1.8 %copy.11 = f32[3,4,12,12,512]{4,1,3,2,0:T(4,128)} copy(f32[3,4,12,12,512]{4,1,3,2,0:T(4,128)S(1)} %bitcast.3) | data formatting | bytes 7077888

commit v5 on v4

--- a/solution.py
+++ b/solution.py
@@ -25,22 +25,60 @@
     return jnp.dot(a, b, preferred_element_type=f32)
 
 
-def attend_window(operand, qkv_weight, scale_row, bias_ref, head_dim, store):
-    tokens, width = operand.shape
+def head_blocks(group, head_dim):
+    d0 = lax.broadcasted_iota(jnp.int32, (group, group), 0)
+    d1 = lax.broadcasted_iota(jnp.int32, (group, group), 1)
+    shift = head_dim.bit_length() - 1
+    same_head = lax.shift_right_logical(d0, shift) == lax.shift_right_logical(d1, shift)
+    return same_head.astype(f32).astype(bf16)
+
+
+def when(condition):
+    if isinstance(condition, bool):
+        return (lambda run: run()) if condition else (lambda run: None)
+    return pl.when(condition)
+
+
+def project_windows(operand, qkv_weight, tokens, head_dim):
+    rows, width = operand.shape
+    group = 4 * head_dim
+    groups = width // group
+    same_head = head_blocks(group, head_dim)
+
+    def project(block, g):
+        at = block * width + g * group
+        return mm(operand, qkv_weight[:, at : at + group])
+
+    def square_sum(part):
+        rounded = part.astype(bf16)
+        return mm(rounded * rounded, same_head)
+
+    raw = [(project(0, g), project(1, g)) for g in range(groups)]
+    sums = [[square_sum(part) for part in raw[g]] for g in range(groups)]
+    value = [project(2, g).astype(bf16) for g in range(groups)]
+    windows = []
+    for at in range(0, rows, tokens):
+        cut = slice(at, at + tokens)
+        windows.append(
+            (
+                [[part[cut] for part in raw[g]] for g in range(groups)],
+                [[part[cut] for part in sums[g]] for g in range(groups)],
+                [part[cut] for part in value],
+            )
+        )
+    return windows
+
+
+def attend_window(projected, scale_row, bias_ref, head_dim, store, between=None):
+    raw, sums, value = projected
+    tokens = value[0].shape[0]
+    width = sum(part.shape[1] for part in value)
     group = 4 * head_dim
     pair = 2 * head_dim
     rest = pair // 4
     main = tokens - rest
     last = (((1,), (1,)), ((), ()))
-    query = mm(operand, qkv_weight[:, :width])
-    key = mm(operand, qkv_weight[:, width : 2 * width])
-    value = mm(operand, qkv_weight[:, 2 * width :]).astype(bf16)
-    d0 = lax.broadcasted_iota(jnp.int32, (group, group), 0)
-    d1 = lax.broadcasted_iota(jnp.int32, (group, group), 1)
-    same_head = lax.shift_right_logical(d0, head_dim.bit_length() - 1) == lax.shift_right_logical(
-        d1, head_dim.bit_length() - 1
-    )
-    same_head = same_head.astype(f32).astype(bf16)
+    groups = width // group
 
     def lanes(rows, cols, at, size):
         lane = lax.broadcasted_iota(jnp.int32, (rows, cols), 1)
@@ -50,25 +88,22 @@
     second_b = lanes(tokens, pair, head_dim, head_dim)
     first = lax.broadcasted_iota(jnp.int32, (tokens, pair), 1) < head_dim
 
-    def unit(part, scale):
-        rounded = part.astype(bf16)
-        inv = lax.rsqrt(mm(rounded * rounded, same_head) + 1e-06)
+    def unit(part, total, scale):
+        inv = lax.rsqrt(total + 1e-06)
         if scale is not None:
             inv = inv * scale
         return (part * inv).astype(bf16)
 
-    for g in range(width // group):
-        at = g * group
-        q = unit(query[:, at : at + group], scale_row[:, at : at + group])
-        k = unit(key[:, at : at + group], None)
-        v = value[:, at : at + group]
+    def rest_shares(q, k):
         k_rest = jnp.concatenate(
             [k[main:] * lanes(rest, group, h * head_dim, head_dim) for h in range(4)], axis=0
         )
-        rest_score = lax.dot_general(q, k_rest, last, preferred_element_type=f32)
+        score = lax.dot_general(q, k_rest, last, preferred_element_type=f32)
         if bias_ref is not None:
-            rest_score = rest_score + bias_ref[:, main:]
-        rest_weights = jnp.exp2(rest_score).astype(bf16)
+            score = score + bias_ref[:, main:]
+        return jnp.exp2(score).astype(bf16)
+
+    def rest_part(weights, v):
         columns = []
         for h in range(4):
             side = h % 2
@@ -76,27 +111,57 @@
             v_rest = v[main:, (h // 2) * pair : (h // 2 + 1) * pair] * own + other
             zero = jnp.zeros_like(v_rest)
             columns.append(jnp.concatenate([v_rest if i == h else zero for i in range(4)], axis=0))
-        rest_out = mm(rest_weights, jnp.concatenate(columns, axis=1))
-        shares = []
+        return mm(weights, jnp.concatenate(columns, axis=1))
+
+    def main_share(q, k, h):
+        cut = slice((h // 2) * pair, (h // 2 + 1) * pair)
+        own = (first_b, second_b)[h % 2][:main]
+        score = lax.dot_general(q[:, cut], k[:main, cut] * own, last, preferred_element_type=f32)
+        if bias_ref is not None:
+            score = score + bias_ref[:, :main]
+        return jnp.exp2(score).astype(bf16)
+
+    def main_part(share, v, h):
+        cut = slice((h // 2) * pair, (h // 2 + 1) * pair)
+        own, other = ((first_b, second_b), (second_b, first_b))[h % 2]
+        return mm(share, v[:main, cut] * own[:main] + other[:main])
+
+    def combine(g, p, even, odd):
+        result = jnp.where(first, even, odd)
+        total = pltpu.roll(jnp.where(first, odd, even), head_dim, 1)
+        at = g * group + p * pair
+        store(slice(at, at + pair), result / total)
+
+    units = [None] * groups
+
+    def scaled(g):
+        at = g * group
+        return (
+            unit(raw[g][0], sums[g][0], scale_row[:, at : at + group]),
+            unit(raw[g][1], sums[g][1], None),
+        )
+
+    units[0] = scaled(0)
+
+    shares = [rest_shares(*units[0])] + [main_share(*units[0], h) for h in range(4)]
+    for g in range(groups):
+        following = g + 1 < groups
+        if following:
+            units[g + 1] = scaled(g + 1)
+        ahead = []
+        rest_out = rest_part(shares[0], value[g])
+        if following:
+            ahead.append(rest_shares(*units[g + 1]))
+        elif between is not None and g > 0:
+            between(g - 1)
+        parts = []
         for h in range(4):
-            cut = slice((h // 2) * pair, (h // 2 + 1) * pair)
-            own = (first_b, second_b)[h % 2][:main]
-            score = lax.dot_general(q[:, cut], k[:main, cut] * own, last, preferred_element_type=f32)
-            if bias_ref is not None:
-                score = score + bias_ref[:, :main]
-            shares.append(jnp.exp2(score).astype(bf16))
-        for p in range(2):
-            cut = slice(p * pair, (p + 1) * pair)
-            v_pair = v[:main, cut]
-            both = []
-            for side, (own, other) in enumerate(((first_b, second_b), (second_b, first_b))):
-                h = 2 * p + side
-                both.append(
-                    mm(shares[h], v_pair * own[:main] + other[:main]) + rest_out[:, h * pair : (h + 1) * pair]
-                )
-            result = jnp.where(first, both[0], both[1])
-            total = pltpu.roll(jnp.where(first, both[1], both[0]), head_dim, 1)
-            store(slice(at + p * pair, at + (p + 1) * pair), (result / total).astype(bf16))
+            parts.append(main_part(shares[1 + h], value[g], h) + rest_out[:, h * pair : (h + 1) * pair])
+            if following:
+                ahead.append(main_share(*units[g + 1], h))
+            if h % 2 == 1:
+                combine(g, h // 2, parts[h - 1], parts[h])
+        shares = ahead
 
 
 def scale_lanes(scale_ref, layer, width, heads):
@@ -122,8 +187,8 @@
     return x * (one + jnp.tanh(inner))
 
 
-def finish_window(x, attended, out_weight, up_ref, down_ref, gain, bias):
-    after = x + norm_rows(mm(attended, out_weight), gain[0:1], bias[0:1])
+def finish_window(x, projected, up_ref, down_ref, gain, bias):
+    after = x + norm_rows(projected, gain[0:1], bias[0:1])
     after_b = after.astype(bf16)
     ff = up_ref.shape[1]
     step = min(512, ff)
@@ -160,21 +225,21 @@
     return key * 3 + band
 
 
-ORDER = "FFFFSSFFSSLLSSLLLL"
-
-
-def order(count):
-    seen = {"F": 0, "S": 0, "L": 0}
+PAIR_F = False
+PAIR_L = (lambda s, n: True)
+
+
+def order(samples, wins):
     plan = []
-    for kind in ORDER:
-        plan.append(("FSL".index(kind), seen[kind]))
-        seen[kind] += 1
-    assert min(seen.values()) == max(seen.values()) == count
+    for k in range(samples + 2):
+        for s, whole, single in ((k, PAIR_F and k > 0, "f"), (k - 1, False, "S"), (k - 2, PAIR_L(k - 2, samples), "l")):
+            if 0 <= s < samples:
+                plan += [(single.upper(), s)] if whole else [(single, s * wins + j) for j in range(wins)]
     return plan
 
 
 def kernel(lat_size, x_hbm, ids_ref, qkv_hbm, out_hbm, up_hbm, down_hbm, gain_ref, bias_ref, scale_ref,
-           x_s, first_s, op_s, att_s, send_s, send_own, back_s, back_own, mask_s, win_f, win_b,
+           x_s, first_s, op_s, att_s, send_s, send_own, back_s, back_own, mask_s, keep_s, win_b,
            scale_s, qkv_s, out_s, up_s, down_s, w_sem, x_sem, send1, recv1, send2, recv2, ids_s, ids_sem):
     samples, lat_rows, lon_cols, levels, width = x_s.shape
     wins = lat_rows // WIN_LAT
@@ -265,63 +330,108 @@
 
     copies = 3 + wins - 1
 
-    def store(cut, value):
-        win_b[:, cut] = value
-
-    def layer_first(i, carry):
-        s, j = lax.div(i, wins), lax.rem(i, wins)
-
-        @pl.when(j == 0)
-        def _():
-            x_load(s).wait()
-
-        @pl.when(i == 0)
-        def _():
-            loads[0][0].wait()
-
-        for half in range(2):
-            for block in range(2):
-                for r in range(HALF_LAT):
-                    row = (half * 2 + block) * quarter + r * run
-                    part = x_s[s, j * WIN_LAT + block * HALF_LAT + r, half * HALF_LON : (half + 1) * HALF_LON]
-                    first_s[i, row : row + run, :] = part.reshape(run, width)
-        attend_window(first_s[i].astype(bf16), qkv_s.at[0], scale_s[0:1, :], None, head_dim, store)
-
-        @pl.when(i == 0)
-        def _():
-            for copy in loads[0][1:]:
-                copy.wait()
-
-        first_s[i] = finish_window(first_s[i], win_b[...], out_s[0], up_s.at[0], down_s.at[0], gain_ref[0], bias_ref[0])
-
-        def block_of(q):
-            return first_s[i, q * quarter : (q + 1) * quarter, :].astype(bf16)
-
-        @pl.when(i == 0)
-        def _():
-            pl.semaphore_wait(barrier, len(peers))
-            ids_copy().start()
-
-        send_s[s, 2 * j] = block_of(2)
-        send_s[s, 2 * j + 1] = block_of(3)
-        op_s[s, 1, 2 * j] = block_of(1)
-
-        @pl.when(j == 0)
-        def _():
-            send_own[s, 0] = block_of(0)
-            for k in range(3):
-                ahead(s, k).start()
-
-        for jj in range(1, wins):
-
-            @pl.when(j == jj)
-            def _():
-                op_s[s, 1, 2 * jj - 1] = block_of(0)
-                ahead(s, 2 + jj).start()
-
-        return carry
-
-    def shifted_attention(i, carry):
+    def layer_first(items, first):
+        for i, s, j in items:
+
+            @when(j == 0)
+            def _():
+                x_load(s).wait()
+
+        if first:
+
+            @pl.when(items[0][0] == 0)
+            def _():
+                loads[0][0].wait()
+
+        for i, s, j in items:
+            for half in range(2):
+                for block in range(2):
+                    for r in range(HALF_LAT):
+                        row = (half * 2 + block) * quarter + r * run
+                        part = x_s[s, j * WIN_LAT + block * HALF_LAT + r, half * HALF_LON : (half + 1) * HALF_LON]
+                        first_s[i, row : row + run, :] = part.reshape(run, width)
+
+        if first:
+
+            @pl.when(items[0][0] == 0)
+            def _():
+                for copy in loads[0][1:]:
+                    copy.wait()
+
+        def residual():
+            return jnp.concatenate([first_s[i] for i, _, _ in items], axis=0)
+
+        rows = len(items) * tokens
+        products = []
+
+        def project(g):
+            cut = slice(g * 4 * head_dim, (g + 1) * 4 * head_dim)
+            products.append(mm(win_b[:rows, cut], out_s[0, cut, :]))
+
+        windows = project_windows(residual().astype(bf16), qkv_s.at[0], tokens, head_dim)
+        for n, window in enumerate(windows):
+
+            def store(cut, value):
+                win_b[n * tokens : (n + 1) * tokens, cut] = value.astype(bf16)
+
+            attend_window(
+                window, scale_s[0:1, :], None, head_dim, store, project if n == len(windows) - 1 else None
+            )
+        project(len(products))
+        total = products[0]
+        for part in products[1:]:
+            total = total + part
+        result = finish_window(residual(), total, up_s.at[0], down_s.at[0], gain_ref[0], bias_ref[0])
+
+        for n, (i, s, j) in enumerate(items):
+            mine = result[n * tokens : (n + 1) * tokens]
+            first_s[i] = mine
+
+            def block_of(q):
+                return mine[q * quarter : (q + 1) * quarter, :].astype(bf16)
+
+            send_s[s, 2 * j] = block_of(2)
+            send_s[s, 2 * j + 1] = block_of(3)
+            op_s[s, 1, 2 * j] = block_of(1)
+            if isinstance(j, int):
+                if j == 0:
+                    send_own[s, 0] = block_of(0)
+                else:
+                    op_s[s, 1, 2 * j - 1] = block_of(0)
+            else:
+                keep_s[...] = block_of(0)
+
+        if first:
+
+            @pl.when(items[0][0] == 0)
+            def _():
+                pl.semaphore_wait(barrier, len(peers))
+                ids_copy().start()
+
+        for i, s, j in items:
+
+            @when(j == 0)
+            def _():
+                if not isinstance(j, int):
+                    send_own[s, 0] = keep_s[...]
+                for k in range(3):
+                    ahead(s, k).start()
+
+            for jj in range(1, wins):
+
+                @when(j == jj)
+                def _():
+                    if not isinstance(j, int):
+                        op_s[s, 1, 2 * jj - 1] = keep_s[...]
+                    ahead(s, 2 + jj).start()
+
+    def first_window(i):
+        layer_first([(i, lax.div(i, wins), lax.rem(i, wins))], True)
+
+    def first_sample(s):
+        layer_first([(s * wins + j, s, j) for j in range(wins)], False)
+
+    def shifted_attention(i):
         s, j = lax.div(i, wins), lax.rem(i, wins)
 
         @pl.when(j == 0)
@@ -345,23 +455,23 @@
             ids_copy().wait_recv()
             make_masks()
 
-        for half in range(2):
-            for block in range(2):
-                row = (half * 2 + block) * quarter
-                win_f[row : row + quarter, :] = op_s[s, half, 2 * j + block].astype(f32)
-        attend_window(win_f[...].astype(bf16), qkv_s.at[1], scale_s[1:2, :], mask_s.at[j], head_dim, store)
-        win_f[...] = win_b[...].astype(f32)
-
-        def block_of(q):
-            return win_f[q * quarter : (q + 1) * quarter, :].astype(bf16)
-
-        att_s[s, 0, 2 * j + 1] = block_of(2)
-        back_s[s, 2 * j] = block_of(0)
-        back_s[s, 2 * j + 1] = block_of(1)
+        operand = jnp.concatenate(
+            [op_s[s, half, 2 * j + block].astype(f32) for half in range(2) for block in range(2)], axis=0
+        ).astype(bf16)
+
+        def store(cut, value):
+            parts = [value[q * quarter : (q + 1) * quarter, :].astype(bf16) for q in range(4)]
+            back_s[s, 2 * j, :, cut] = parts[0]
+            back_s[s, 2 * j + 1, :, cut] = parts[1]
+            att_s[s, 0, 2 * j + 1, :, cut] = parts[2]
+            keep_s[:, cut] = parts[3]
+
+        window = project_windows(operand, qkv_s.at[1], tokens, head_dim)[0]
+        attend_window(window, scale_s[1:2, :], mask_s.at[j], head_dim, store)
 
         @pl.when(j == wins - 1)
         def _():
-            back_own[s, 0] = block_of(3)
+            back_own[s, 0] = keep_s[...]
             for k in range(3):
                 back(s, k).start()
 
@@ -369,51 +479,58 @@
 
             @pl.when(j == jj)
             def _():
-                att_s[s, 0, 2 * jj + 2] = block_of(3)
+                att_s[s, 0, 2 * jj + 2] = keep_s[...]
                 back(s, 3 + jj).start()
 
-        return carry
-
-    def layer_last(i, carry):
-        s, j = lax.div(i, wins), lax.rem(i, wins)
-
-        @pl.when(j == 0)
-        def _():
-            for k in (1, 2):
-                back(s, k).wait_recv()
-
-        for jj in range(wins - 1):
-
-            @pl.when(j == jj)
-            def _():
-                back(s, 3 + jj).wait_recv()
-
-        @pl.when(j == wins - 1)
-        def _():
-            back(s, 0).wait_recv()
-
-        @pl.when(i == 0)
+    def layer_last(items):
+        for i, s, j in items:
+
+            @when(j == 0)
+            def _():
+                for k in (1, 2):
+                    back(s, k).wait_recv()
+
+            for jj in range(wins - 1):
+
+                @when(j == jj)
+                def _():
+                    back(s, 3 + jj).wait_recv()
+
+            @when(j == wins - 1)
+            def _():
+                back(s, 0).wait_recv()
+
+        @pl.when(items[0][0] == 0)
         def _():
             for copy in loads[1][1:]:
                 copy.wait()
 
-        for half in range(2):
-            for block in range(2):
-                row = (half * 2 + block) * quarter
-                win_f[row : row + quarter, :] = att_s[s, half, 2 * j + block].astype(f32)
-        win_f[...] = finish_window(
-            first_s[i], win_f[...].astype(bf16), out_s[1], up_s.at[1], down_s.at[1], gain_ref[1], bias_ref[1]
+        attended = jnp.concatenate(
+            [att_s[s, half, 2 * j + block].astype(f32) for _, s, j in items for half in range(2) for block in range(2)],
+            axis=0,
+        ).astype(bf16)
+        result = finish_window(
+            jnp.concatenate([first_s[i] for i, _, _ in items], axis=0),
+            mm(attended, out_s[1]), up_s.at[1], down_s.at[1], gain_ref[1], bias_ref[1],
         )
-        for half in range(2):
-            for block in range(2):
-                for r in range(HALF_LAT):
-                    row = (half * 2 + block) * quarter + r * run
-                    x_s[s, j * WIN_LAT + block * HALF_LAT + r, half * HALF_LON : (half + 1) * HALF_LON] = win_f[
-                        row : row + run, :
-                    ].reshape(HALF_LON, levels, width)
-        return carry
-
-    plan = order(samples * wins)
+        for n, (_, s, j) in enumerate(items):
+            for half in range(2):
+                for block in range(2):
+                    for r in range(HALF_LAT):
+                        row = n * tokens + (half * 2 + block) * quarter + r * run
+                        x_s[s, j * WIN_LAT + block * HALF_LAT + r, half * HALF_LON : (half + 1) * HALF_LON] = result[
+                            row : row + run, :
+                        ].reshape(HALF_LON, levels, width)
+
+    def last_window(i):
+        layer_last([(i, lax.div(i, wins), lax.rem(i, wins))])
+
+    def last_sample(s):
+        layer_last([(s * wins + j, s, j) for j in range(wins)])
+
+    plan = order(samples, wins)
+    steps = {"f": first_window, "F": first_sample, "S": shifted_attention, "l": last_window, "L": last_sample}
+    kinds = [kind for kind in steps if any(kind == k for k, _ in plan)]
 
     def pick(t, values):
         value = jnp.int32(values[0])
@@ -423,13 +540,13 @@
         return value
 
     def advance(t, carry):
-        kind = pick(t, [k for k, _ in plan])
-        i = pick(t, [n for _, n in plan])
-        for k, step in enumerate((layer_first, shifted_attention, layer_last)):
+        kind = pick(t, [kinds.index(k) for k, _ in plan])
+        n = pick(t, [n for _, n in plan])
+        for k, name in enumerate(kinds):
 
             @pl.when(kind == k)
             def _():
-                step(i, 0)
+                steps[name](n)
 
         return carry
 
@@ -473,8 +590,8 @@
             pltpu.VMEM((samples, blocks, quarter, width), bf16),
             pltpu.VMEM((samples, 1, quarter, width), bf16),
             pltpu.VMEM((wins, tokens, tokens + 3 * (width // logit_scale.shape[1] // 2)), f32),
-            pltpu.VMEM((tokens, width), f32),
-            pltpu.VMEM((tokens, width), bf16),
+            pltpu.VMEM((quarter, width), bf16),
+            pltpu.VMEM((wins * tokens, width), bf16),
             pltpu.VMEM((2, width), f32),
             pltpu.VMEM(qkv_weight.shape, bf16),
             pltpu.VMEM(out_weight.shape, bf16),

time: 65.6 us -> 62.3 us (0.950)
  Pallas kernels: 63.6 us -> 60.3 us
    pallas_call x1, Pallas kernels: 63.6 us -> 60.3 us  [local(): pl.pallas_call(functools.partial(kernel, lax.axis_size('lat')), in_specs=...]
where the time goes in v5:
time: 62.3 us; the launch traced here: 62.1 us
  Pallas kernels  60.3 us (97%)
  local copies, waits for them, and re-layouts  1.8 us (3%)
    pallas_call x1, Pallas kernels, local(): pl.pallas_call(functools.partial(kernel, lax.axis_size('lat')), in_specs=...  60.3 us
    unnamed x1, local copies, waits for them, and re-layouts  1.8 us

profile of v5, /device:TPU:1, one launch (start us, length us, event | category | flops | bytes accessed | tf_op | source)
XLA Modules:
  0.0 62.1 jit_solution(9628930681070543088)
XLA Ops:
  0.0 60.3 %both_layers.1 = f32[3,12,12,4,512]{4,3,2,1,0:T(4,128)S(1)} custom-call(f32[3,12,12,4,512]{4,3,2,1,0:T(4,128)} %bitcast.4, s32[12,4,12]{2,1,0:T(4,128)} %bitcast.5, bf16[2,512,1536]{2,1,0:T(8,128)(2,1)} %qkv_hbm.1, bf16[2,512,512]{2,1,0:T(8,128)(2,1)} %out_hbm.1, bf16[2,512,2048]{2,1,0:T(8,128)(2,1)} %up_hbm.1, bf16[2,2048,512]{2,1,0:T(8,128)(2,1)} %down_hbm.1, ...), custom_call_target="tpu_custom_call" | custom-call | tf_op jit(solution)/shard_map/both_layers/pallas_call | solution.py:579
  60.3 1.8 %copy.11 = f32[3,4,12,12,512]{4,1,3,2,0:T(4,128)} copy(f32[3,4,12,12,512]{4,1,3,2,0:T(4,128)S(1)} %bitcast.3) | data formatting | bytes 7077888

commit v6 on v5

--- a/solution.py
+++ b/solution.py
@@ -225,16 +225,19 @@
     return key * 3 + band
 
 
-PAIR_F = False
-PAIR_L = (lambda s, n: True)
+PAIR_LAST = False
 
 
 def order(samples, wins):
     plan = []
     for k in range(samples + 2):
-        for s, whole, single in ((k, PAIR_F and k > 0, "f"), (k - 1, False, "S"), (k - 2, PAIR_L(k - 2, samples), "l")):
+        for s, kind in ((k, "f"), (k - 1, "S"), (k - 2, "l")):
             if 0 <= s < samples:
-                plan += [(single.upper(), s)] if whole else [(single, s * wins + j) for j in range(wins)]
+                if kind == "l" and (s < samples - 1 or PAIR_LAST):
+                    plan.append(("L", s))
+                else:
+                    plan += [(kind, s * wins + j) for j in range(wins)]
+    plan[0] = ("a", 0)
     return plan
 
 
@@ -258,14 +261,17 @@
         for layer in range(2)
     ]
 
-    def x_load(s):
-        return pltpu.make_async_copy(x_hbm.at[s], x_s.at[s], x_sem.at[s])
-
-    x_load(0).start()
+    def x_load(s, j):
+        rows = pl.ds(j * WIN_LAT, WIN_LAT)
+        return pltpu.make_async_copy(x_hbm.at[s, rows], x_s.at[s, rows], x_sem.at[s, j])
+
+    x_load(0, 0).start()
     for copy in loads[0]:
         copy.start()
-    for s in range(1, samples):
-        x_load(s).start()
+    for s in range(samples):
+        for j in range(wins):
+            if s + j > 0:
+                x_load(s, j).start()
     for copy in loads[1]:
         copy.start()
 
@@ -332,16 +338,9 @@
 
     def layer_first(items, first):
         for i, s, j in items:
-
-            @when(j == 0)
-            def _():
-                x_load(s).wait()
-
+            x_load(s, j).wait()
         if first:
-
-            @pl.when(items[0][0] == 0)
-            def _():
-                loads[0][0].wait()
+            loads[0][0].wait()
 
         for i, s, j in items:
             for half in range(2):
@@ -351,13 +350,6 @@
                         part = x_s[s, j * WIN_LAT + block * HALF_LAT + r, half * HALF_LON : (half + 1) * HALF_LON]
                         first_s[i, row : row + run, :] = part.reshape(run, width)
 
-        if first:
-
-            @pl.when(items[0][0] == 0)
-            def _():
-                for copy in loads[0][1:]:
-                    copy.wait()
-
         def residual():
             return jnp.concatenate([first_s[i] for i, _, _ in items], axis=0)
 
@@ -375,9 +367,18 @@
                 win_b[n * tokens : (n + 1) * tokens, cut] = value.astype(bf16)
 
             attend_window(
-                window, scale_s[0:1, :], None, head_dim, store, project if n == len(windows) - 1 else None
+                window,
+                scale_s[0:1, :],
+                None,
+                head_dim,
+                store,
+                project if n == len(windows) - 1 and not first else None,
             )
-        project(len(products))
+        if first:
+            for copy in loads[0][1:]:
+                copy.wait()
+        while len(products) * 4 * head_dim < width:
+            project(len(products))
         total = products[0]
         for part in products[1:]:
             total = total + part
@@ -402,11 +403,8 @@
                 keep_s[...] = block_of(0)
 
         if first:
-
-            @pl.when(items[0][0] == 0)
-            def _():
-                pl.semaphore_wait(barrier, len(peers))
-                ids_copy().start()
+            pl.semaphore_wait(barrier, len(peers))
+            ids_copy().start()
 
         for i, s, j in items:
 
@@ -425,8 +423,11 @@
                         op_s[s, 1, 2 * jj - 1] = keep_s[...]
                     ahead(s, 2 + jj).start()
 
+    def opening(i):
+        layer_first([(0, 0, 0)], True)
+
     def first_window(i):
-        layer_first([(i, lax.div(i, wins), lax.rem(i, wins))], True)
+        layer_first([(i, lax.div(i, wins), lax.rem(i, wins))], False)
 
     def first_sample(s):
         layer_first([(s * wins + j, s, j) for j in range(wins)], False)
@@ -472,7 +473,7 @@
         @pl.when(j == wins - 1)
         def _():
             back_own[s, 0] = keep_s[...]
-            for k in range(3):
+            for k in (1, 0, 2):
                 back(s, k).start()
 
         for jj in range(wins - 1):
@@ -529,7 +530,7 @@
         layer_last([(s * wins + j, s, j) for j in range(wins)])
 
     plan = order(samples, wins)
-    steps = {"f": first_window, "F": first_sample, "S": shifted_attention, "l": last_window, "L": last_sample}
+    steps = {"a": opening, "f": first_window, "F": first_sample, "S": shifted_attention, "l": last_window, "L": last_sample}
     kinds = [kind for kind in steps if any(kind == k for k, _ in plan)]
 
     def pick(t, values):
@@ -598,7 +599,7 @@
             pltpu.VMEM(up_weight.shape, bf16),
             pltpu.VMEM(down_weight.shape, bf16),
             sem((2, 4)),
-            sem((samples,)),
+            sem((samples, wins)),
             sem((samples, copies)),
             sem((samples, copies)),
             sem((samples, copies)),

time: 62.3 us -> 60.5 us (0.971)
  Pallas kernels: 60.3 us -> 58.5 us
    pallas_call x1, Pallas kernels: 60.3 us -> 58.5 us  [local(): pl.pallas_call(functools.partial(kernel, lax.axis_size('lat')), in_specs=...]
where the time goes in v6:
time: 60.5 us; the launch traced here: 60.3 us
  Pallas kernels  58.5 us (97%)
  local copies, waits for them, and re-layouts  1.8 us (3%)
    pallas_call x1, Pallas kernels, local(): pl.pallas_call(functools.partial(kernel, lax.axis_size('lat')), in_specs=...  58.5 us
    unnamed x1, local copies, waits for them, and re-layouts  1.8 us

profile of v6, /device:TPU:1, one launch (start us, length us, event | category | flops | bytes accessed | tf_op | source)
XLA Modules:
  0.0 60.3 jit_solution(11356638629951075671)
XLA Ops:
  0.0 58.5 %both_layers.1 = f32[3,12,12,4,512]{4,3,2,1,0:T(4,128)S(1)} custom-call(f32[3,12,12,4,512]{4,3,2,1,0:T(4,128)} %bitcast.4, s32[12,4,12]{2,1,0:T(4,128)} %bitcast.5, bf16[2,512,1536]{2,1,0:T(8,128)(2,1)} %qkv_hbm.1, bf16[2,512,512]{2,1,0:T(8,128)(2,1)} %out_hbm.1, bf16[2,512,2048]{2,1,0:T(8,128)(2,1)} %up_hbm.1, bf16[2,2048,512]{2,1,0:T(8,128)(2,1)} %down_hbm.1, ...), custom_call_target="tpu_custom_call" | custom-call | tf_op jit(solution)/shard_map/both_layers/pallas_call | solution.py:580
  58.5 1.8 %copy.11 = f32[3,4,12,12,512]{4,1,3,2,0:T(4,128)} copy(f32[3,4,12,12,512]{4,1,3,2,0:T(4,128)S(1)} %bitcast.3) | data formatting | bytes 7077888

commit v7 on v6

--- a/solution.py
+++ b/solution.py
@@ -12,7 +12,8 @@
 HALF_LAT = WIN_LAT // 2
 HALF_LON = WIN_LON // 2
 LOG2E = 1.4426950408889634
-VMEM_LIMIT = 60 * 1024 * 1024
+VMEM_LIMIT = 51 * 1024 * 1024 + 512 * 1024
+CLOSING_LIMIT = 40 * 1024 * 1024
 
 f32 = jnp.float32
 bf16 = jnp.bfloat16
@@ -225,24 +226,21 @@
     return key * 3 + band
 
 
-PAIR_LAST = False
-
-
 def order(samples, wins):
     plan = []
     for k in range(samples + 2):
         for s, kind in ((k, "f"), (k - 1, "S"), (k - 2, "l")):
             if 0 <= s < samples:
-                if kind == "l" and (s < samples - 1 or PAIR_LAST):
+                if kind == "l" and s < samples - 1:
                     plan.append(("L", s))
                 else:
                     plan += [(kind, s * wins + j) for j in range(wins)]
     plan[0] = ("a", 0)
-    return plan
+    return plan[:-1]
 
 
 def kernel(lat_size, x_hbm, ids_ref, qkv_hbm, out_hbm, up_hbm, down_hbm, gain_ref, bias_ref, scale_ref,
-           x_s, first_s, op_s, att_s, send_s, send_own, back_s, back_own, mask_s, keep_s, win_b,
+           x_s, first_o, att_o, out1_s, up1_s, down1_s, first_s, op_s, att_s, send_s, send_own, back_s, back_own, mask_s, keep_s, win_b,
            scale_s, qkv_s, out_s, up_s, down_s, w_sem, x_sem, send1, recv1, send2, recv2, ids_s, ids_sem):
     samples, lat_rows, lon_cols, levels, width = x_s.shape
     wins = lat_rows // WIN_LAT
@@ -253,12 +251,12 @@
 
     loads = [
         [
-            pltpu.make_async_copy(src.at[layer], dst.at[layer], w_sem.at[layer, k])
-            for k, (src, dst) in enumerate(
-                ((qkv_hbm, qkv_s), (out_hbm, out_s), (up_hbm, up_s), (down_hbm, down_s))
-            )
+            pltpu.make_async_copy(src.at[layer], dst, w_sem.at[layer, k])
+            for k, (src, dst) in enumerate(zip((qkv_hbm, out_hbm, up_hbm, down_hbm), targets))
         ]
-        for layer in range(2)
+        for layer, targets in enumerate(
+            ((qkv_s.at[0], out_s, up_s, down_s), (qkv_s.at[1], out1_s, up1_s, down1_s))
+        )
     ]
 
     def x_load(s, j):
@@ -358,7 +356,7 @@
 
         def project(g):
             cut = slice(g * 4 * head_dim, (g + 1) * 4 * head_dim)
-            products.append(mm(win_b[:rows, cut], out_s[0, cut, :]))
+            products.append(mm(win_b[:rows, cut], out_s[cut, :]))
 
         windows = project_windows(residual().astype(bf16), qkv_s.at[0], tokens, head_dim)
         for n, window in enumerate(windows):
@@ -382,7 +380,7 @@
         total = products[0]
         for part in products[1:]:
             total = total + part
-        result = finish_window(residual(), total, up_s.at[0], down_s.at[0], gain_ref[0], bias_ref[0])
+        result = finish_window(residual(), total, up_s, down_s, gain_ref[0], bias_ref[0])
 
         for n, (i, s, j) in enumerate(items):
             mine = result[n * tokens : (n + 1) * tokens]
@@ -512,7 +510,7 @@
         ).astype(bf16)
         result = finish_window(
             jnp.concatenate([first_s[i] for i, _, _ in items], axis=0),
-            mm(attended, out_s[1]), up_s.at[1], down_s.at[1], gain_ref[1], bias_ref[1],
+            mm(attended, out1_s[...]), up1_s, down1_s, gain_ref[1], bias_ref[1],
         )
         for n, (_, s, j) in enumerate(items):
             for half in range(2):
@@ -553,6 +551,18 @@
 
     lax.fori_loop(0, len(plan), advance, 0)
 
+    if samples * wins == 1:
+        for copy in loads[1][1:]:
+            copy.wait()
+    if wins == 1:
+        for k in (1, 2):
+            back(samples - 1, k).wait_recv()
+    back(samples - 1, 0).wait_recv()
+    first_o[...] = first_s[samples * wins - 1]
+    for half in range(2):
+        for block in range(2):
+            att_o[half, block] = att_s[samples - 1, half, blocks - 2 + block]
+
     def drain(s, carry):
         for k in range(copies):
             ahead(s, k).wait_send()
@@ -561,6 +571,42 @@
 
     lax.fori_loop(0, samples, drain, 0)
     ids_copy().wait_send()
+
+
+def closing(x_ref, first_ref, att_ref, out_ref, up_ref, down_ref, gain_ref, bias_ref, y_hbm, last_s, sems):
+    samples, lat_rows, lon_cols, levels, width = x_ref.shape
+    wins = lat_rows // WIN_LAT
+    run = HALF_LON * levels
+    quarter = HALF_LAT * run
+
+    def store(src, s, j):
+        return pltpu.make_async_copy(src, y_hbm.at[s, pl.ds(j * WIN_LAT, WIN_LAT)], sems.at[s, j])
+
+    copies = [
+        store(x_ref.at[s, pl.ds(j * WIN_LAT, WIN_LAT)], s, j)
+        for s in range(samples)
+        for j in range(wins)
+        if s * wins + j < samples * wins - 1
+    ]
+    for copy in copies:
+        copy.start()
+    attended = jnp.concatenate(
+        [att_ref[half, block].astype(f32) for half in range(2) for block in range(2)], axis=0
+    ).astype(bf16)
+    result = finish_window(
+        first_ref[...], mm(attended, out_ref[...]), up_ref, down_ref, gain_ref[1], bias_ref[1]
+    )
+    for half in range(2):
+        for block in range(2):
+            for r in range(HALF_LAT):
+                row = (half * 2 + block) * quarter + r * run
+                last_s[block * HALF_LAT + r, half * HALF_LON : (half + 1) * HALF_LON] = result[
+                    row : row + run, :
+                ].reshape(HALF_LON, levels, width)
+    copies.append(store(last_s, samples - 1, wins - 1))
+    copies[-1].start()
+    for copy in copies:
+        copy.wait()
 
 
 def local(stream, region_ids, qkv_weight, out_weight, up_weight, down_weight, norm_gain, norm_bias, logit_scale):
@@ -577,11 +623,19 @@
     vmem = pl.BlockSpec(memory_space=pltpu.VMEM)
     smem = pl.BlockSpec(memory_space=pltpu.SMEM)
     sem = pltpu.SemaphoreType.DMA
-    y = pl.pallas_call(
+    handed = [
+        pltpu.VMEM(x.shape, f32),
+        pltpu.VMEM((tokens, width), f32),
+        pltpu.VMEM((2, 2, quarter, width), bf16),
+        pltpu.VMEM(out_weight.shape[1:], bf16),
+        pltpu.VMEM(up_weight.shape[1:], bf16),
+        pltpu.VMEM(down_weight.shape[1:], bf16),
+    ]
+    parts = pl.pallas_call(
         functools.partial(kernel, lax.axis_size("lat")),
         in_specs=[hbm, vmem, hbm, hbm, hbm, hbm, vmem, vmem, smem],
-        out_specs=vmem,
-        out_shape=pltpu.VMEM(x.shape, f32),
+        out_specs=[vmem] * len(handed),
+        out_shape=handed,
         scratch_shapes=[
             pltpu.VMEM((samples * wins, tokens, width), f32),
             pltpu.VMEM((samples, 2, blocks, quarter, width), bf16),
@@ -595,9 +649,9 @@
             pltpu.VMEM((wins * tokens, width), bf16),
             pltpu.VMEM((2, width), f32),
             pltpu.VMEM(qkv_weight.shape, bf16),
-            pltpu.VMEM(out_weight.shape, bf16),
-            pltpu.VMEM(up_weight.shape, bf16),
-            pltpu.VMEM(down_weight.shape, bf16),
+            pltpu.VMEM(out_weight.shape[1:], bf16),
+            pltpu.VMEM(up_weight.shape[1:], bf16),
+            pltpu.VMEM(down_weight.shape[1:], bf16),
             sem((2, 4)),
             sem((samples, wins)),
             sem((samples, copies)),
@@ -612,6 +666,15 @@
         ),
         name="both_layers",
     )(x, ids, qkv_weight, out_weight, up_weight, down_weight, norm_gain, norm_bias, logit_scale)
+    y = pl.pallas_call(
+        closing,
+        in_specs=[vmem] * (len(handed) + 2),
+        out_specs=hbm,
+        out_shape=jax.ShapeDtypeStruct(x.shape, f32),
+        scratch_shapes=[pltpu.VMEM((WIN_LAT,) + x.shape[2:], f32), sem((samples, wins))],
+        compiler_params=pltpu.CompilerParams(vmem_limit_bytes=CLOSING_LIMIT),
+        name="closing",
+    )(*[pltpu.with_memory_space_constraint(part, pltpu.VMEM) for part in parts], norm_gain, norm_bias)
     return y.transpose(0, 3, 1, 2, 4)
 
 

time: 60.5 us -> 59.6 us (0.985)
  local copies, waits for them, and re-layouts: 1.8 us -> 0.01 us
  Pallas kernels: 58.5 us -> 59.4 us
    pallas_call x0 -> x1, Pallas kernels: none -> 3.17 us  [local(): pl.pallas_call(closing, in_specs=[vmem] * (len(handed) + 2), out_specs=hb...]
    pallas_call x1, Pallas kernels: 58.5 us -> 56.3 us  [local(): pl.pallas_call(functools.partial(kernel, lax.axis_size('lat')), in_specs=...]
    unnamed x1 -> x4, local copies, waits for them, and re-layouts: 1.8 us -> 0.01 us
where the time goes in v7:
time: 59.6 us; the launch traced here: 59.5 us
  Pallas kernels  59.4 us (100%)
    pallas_call x1, Pallas kernels, local(): pl.pallas_call(functools.partial(kernel, lax.axis_size('lat')), in_specs=...  56.3 us
    pallas_call x1, Pallas kernels, local(): pl.pallas_call(closing, in_specs=[vmem] * (len(handed) + 2), out_specs=hb...  3.17 us

profile of v7, /device:TPU:1, one launch (start us, length us, event | category | flops | bytes accessed | tf_op | source)
XLA Modules:
  0.0 59.5 jit_solution(9848943130753433869)
XLA Ops:
  0.0 0.0 copy-start
  0.0 0.0 copy-start.1
  0.0 56.3 %both_layers.1 = (f32[3,12,12,4,512]{4,3,2,1,0:T(4,128)S(1)}, f32[288,512]{1,0:T(8,128)S(1)}, bf16[2,2,72,512]{3,2,1,0:T(8,128)(2,1)S(1)}, bf16[512,512]{1,0:T(8...) custom-call(f32[3,12,12,4,512]{4,3,2,1,0:T(4,128)} %bitcast.3, s32[12,4,12]{2,1,0:T(4,128)} %bitcast.4, ...), custom_call_target="tpu_custom_call" | custom-call | tf_op jit(solution)/shard_map/both_layers/pallas_call | solution.py:634
  56.3 0.0 copy-done
  56.3 0.0 copy-done.1
  56.3 3.2 %closing.1 = f32[3,12,12,4,512]{4,3,2,1,0:T(4,128)} custom-call(f32[3,12,12,4,512]{4,3,2,1,0:T(4,128)S(1)} %get-tuple-element.11.x_ref, f32[288,512]{1,0:T(8,128)S(1)} %get-tuple-element.12.first_ref, bf16[2,2,72,512]{3,2,1,0:T(8,128)(2,1)S(1)} %get-tuple-element.13.att_ref, bf16[512,512]{1,0:T(8,128)(2,1)S(1)} %get-tuple-element.14.out_ref, ...), custom_call_target="tpu_custom_call" | custom-call | tf_op jit(solution)/shard_map/closing/pallas_call | solution.py:669
Async XLA Ops:
  0.0 56.3 %copy-start = (f32[2,2,512]{2,1,0:T(2,128)S(1)}, f32[2,2,512]{2,1,0:T(2,128)}, u32[]{:S(2)}) copy-start(f32[2,2,512]{2,1,0:T(2,128)} %gain_ref.3) | copy-start | bytes 24580
  0.0 56.3 %copy-start.1 = (f32[2,2,512]{2,1,0:T(2,128)S(1)}, f32[2,2,512]{2,1,0:T(2,128)}, u32[]{:S(2)}) copy-start(f32[2,2,512]{2,1,0:T(2,128)} %bias_ref.3) | copy-start | bytes 24580

commit v8 on v7

--- a/solution.py
+++ b/solution.py
@@ -40,7 +40,7 @@
     return pl.when(condition)
 
 
-def project_windows(operand, qkv_weight, tokens, head_dim):
+def project_windows(operand, qkv_weight, tokens, head_dim, joint):
     rows, width = operand.shape
     group = 4 * head_dim
     groups = width // group
@@ -50,12 +50,16 @@
         at = block * width + g * group
         return mm(operand, qkv_weight[:, at : at + group])
 
-    def square_sum(part):
+    def square(part):
         rounded = part.astype(bf16)
-        return mm(rounded * rounded, same_head)
+        return rounded * rounded
 
     raw = [(project(0, g), project(1, g)) for g in range(groups)]
-    sums = [[square_sum(part) for part in raw[g]] for g in range(groups)]
+    if joint:
+        every = mm(jnp.concatenate([square(part) for g in range(groups) for part in raw[g]], axis=0), same_head)
+        sums = [[every[(2 * g + n) * rows : (2 * g + n + 1) * rows] for n in range(2)] for g in range(groups)]
+    else:
+        sums = [[mm(square(part), same_head) for part in raw[g]] for g in range(groups)]
     value = [project(2, g).astype(bf16) for g in range(groups)]
     windows = []
     for at in range(0, rows, tokens):
@@ -358,7 +362,7 @@
             cut = slice(g * 4 * head_dim, (g + 1) * 4 * head_dim)
             products.append(mm(win_b[:rows, cut], out_s[cut, :]))
 
-        windows = project_windows(residual().astype(bf16), qkv_s.at[0], tokens, head_dim)
+        windows = project_windows(residual().astype(bf16), qkv_s.at[0], tokens, head_dim, True)
         for n, window in enumerate(windows):
 
             def store(cut, value):
@@ -465,7 +469,7 @@
             att_s[s, 0, 2 * j + 1, :, cut] = parts[2]
             keep_s[:, cut] = parts[3]
 
-        window = project_windows(operand, qkv_s.at[1], tokens, head_dim)[0]
+        window = project_windows(operand, qkv_s.at[1], tokens, head_dim, False)[0]
         attend_window(window, scale_s[1:2, :], mask_s.at[j], head_dim, store)
 
         @pl.when(j == wins - 1)

time: 59.6 us -> 58.1 us (0.975)
  Pallas kernels: 59.4 us -> 57.9 us
    pallas_call x1, Pallas kernels: 56.3 us -> 54.8 us  [local(): pl.pallas_call(functools.partial(kernel, lax.axis_size('lat')), in_specs=...]
where the time goes in v8:
time: 58.1 us; the launch traced here: 58 us
  Pallas kernels  57.9 us (100%)
    pallas_call x1, Pallas kernels, local(): pl.pallas_call(functools.partial(kernel, lax.axis_size('lat')), in_specs=...  54.8 us
    pallas_call x1, Pallas kernels, local(): pl.pallas_call(closing, in_specs=[vmem] * (len(handed) + 2), out_specs=hb...  3.17 us

profile of v8, /device:TPU:1, one launch (start us, length us, event | category | flops | bytes accessed | tf_op | source)
XLA Modules:
  0.0 58.0 jit_solution(6184093395632585343)
XLA Ops:
  0.0 0.0 copy-start
  0.0 0.0 copy-start.1
  0.0 54.8 %both_layers.1 = (f32[3,12,12,4,512]{4,3,2,1,0:T(4,128)S(1)}, f32[288,512]{1,0:T(8,128)S(1)}, bf16[2,2,72,512]{3,2,1,0:T(8,128)(2,1)S(1)}, bf16[512,512]{1,0:T(8...) custom-call(f32[3,12,12,4,512]{4,3,2,1,0:T(4,128)} %bitcast.3, s32[12,4,12]{2,1,0:T(4,128)} %bitcast.4, ...), custom_call_target="tpu_custom_call" | custom-call | tf_op jit(solution)/shard_map/both_layers/pallas_call | solution.py:638
  54.8 0.0 copy-done
  54.8 0.0 copy-done.1
  54.8 3.2 %closing.1 = f32[3,12,12,4,512]{4,3,2,1,0:T(4,128)} custom-call(f32[3,12,12,4,512]{4,3,2,1,0:T(4,128)S(1)} %get-tuple-element.11.x_ref, f32[288,512]{1,0:T(8,128)S(1)} %get-tuple-element.12.first_ref, bf16[2,2,72,512]{3,2,1,0:T(8,128)(2,1)S(1)} %get-tuple-element.13.att_ref, bf16[512,512]{1,0:T(8,128)(2,1)S(1)} %get-tuple-element.14.out_ref, ...), custom_call_target="tpu_custom_call" | custom-call | tf_op jit(solution)/shard_map/closing/pallas_call | solution.py:673
Async XLA Ops:
  0.0 54.8 %copy-start = (f32[2,2,512]{2,1,0:T(2,128)S(1)}, f32[2,2,512]{2,1,0:T(2,128)}, u32[]{:S(2)}) copy-start(f32[2,2,512]{2,1,0:T(2,128)} %gain_ref.3) | copy-start | bytes 24580
  0.0 54.8 %copy-start.1 = (f32[2,2,512]{2,1,0:T(2,128)S(1)}, f32[2,2,512]{2,1,0:T(2,128)}, u32[]{:S(2)}) copy-start(f32[2,2,512]{2,1,0:T(2,128)} %bias_ref.3) | copy-start | bytes 24580

commit v9 on v8

--- a/solution.py
+++ b/solution.py
@@ -197,11 +197,8 @@
     after_b = after.astype(bf16)
     ff = up_ref.shape[1]
     step = min(512, ff)
-    total = None
-    for at in range(0, ff, step):
-        hidden = gelu_twice(mm(after_b, up_ref[:, at : at + step]))
-        part = mm(hidden, down_ref[at : at + step, :])
-        total = part if total is None else total + part
+    hidden = [gelu_twice(mm(after_b, up_ref[:, at : at + step])) for at in range(0, ff, step)]
+    total = mm(jnp.concatenate(hidden, axis=1), down_ref[...])
     return after + norm_rows(0.5 * total, gain[1:2], bias[1:2])
 
 

time: 58.1 us -> 57.4 us (0.988)
  Pallas kernels: 57.9 us -> 57 us
    pallas_call x1, Pallas kernels: 54.8 us -> 54.1 us  [local(): pl.pallas_call(functools.partial(kernel, lax.axis_size('lat')), in_specs=...]
where the time goes in v9:
time: 57.4 us; the launch traced here: 57 us
  Pallas kernels  57 us (99%)
    pallas_call x1, Pallas kernels, local(): pl.pallas_call(functools.partial(kernel, lax.axis_size('lat')), in_specs=...  54.1 us
    pallas_call x1, Pallas kernels, local(): pl.pallas_call(closing, in_specs=[vmem] * (len(handed) + 2), out_specs=hb...  2.94 us

profile of v9, /device:TPU:1, one launch (start us, length us, event | category | flops | bytes accessed | tf_op | source)
XLA Modules:
  0.0 57.0 jit_solution(4734132994145774703)
XLA Ops:
  0.0 0.0 copy-start
  0.0 0.0 copy-start.1
  0.0 54.1 %both_layers.1 = (f32[3,12,12,4,512]{4,3,2,1,0:T(4,128)S(1)}, f32[288,512]{1,0:T(8,128)S(1)}, bf16[2,2,72,512]{3,2,1,0:T(8,128)(2,1)S(1)}, bf16[512,512]{1,0:T(8...) custom-call(f32[3,12,12,4,512]{4,3,2,1,0:T(4,128)} %bitcast.3, s32[12,4,12]{2,1,0:T(4,128)} %bitcast.4, ...), custom_call_target="tpu_custom_call" | custom-call | tf_op jit(solution)/shard_map/both_layers/pallas_call | solution.py:635
  54.1 0.0 copy-done
  54.1 0.0 copy-done.1
  54.1 2.9 %closing.1 = f32[3,12,12,4,512]{4,3,2,1,0:T(4,128)} custom-call(f32[3,12,12,4,512]{4,3,2,1,0:T(4,128)S(1)} %get-tuple-element.11.x_ref, f32[288,512]{1,0:T(8,128)S(1)} %get-tuple-element.12.first_ref, bf16[2,2,72,512]{3,2,1,0:T(8,128)(2,1)S(1)} %get-tuple-element.13.att_ref, bf16[512,512]{1,0:T(8,128)(2,1)S(1)} %get-tuple-element.14.out_ref, ...), custom_call_target="tpu_custom_call" | custom-call | tf_op jit(solution)/shard_map/closing/pallas_call | solution.py:670
Async XLA Ops:
  0.0 54.1 %copy-start = (f32[2,2,512]{2,1,0:T(2,128)S(1)}, f32[2,2,512]{2,1,0:T(2,128)}, u32[]{:S(2)}) copy-start(f32[2,2,512]{2,1,0:T(2,128)} %gain_ref.3) | copy-start | bytes 24580
  0.0 54.1 %copy-start.1 = (f32[2,2,512]{2,1,0:T(2,128)S(1)}, f32[2,2,512]{2,1,0:T(2,128)}, u32[]{:S(2)}) copy-start(f32[2,2,512]{2,1,0:T(2,128)} %bias_ref.3) | copy-start | bytes 24580
